TPU v7x, 512 devices: a whole 4x8x8 slice. The times are simulated.
512 devices in a mesh: ctx: 64 (over z, y_hi, core), head: 8 (over x, y_lo).
Axes of the slice: x: 4, y: 8 (y_hi: 4, y_lo: 2; y = y_hi * 2 + y_lo), z: 8, core: 2. Of those that a mesh axis runs over, the one named last changes fastest.
Arguments:
- prompt_latent: bfloat16 [6144, 576], P('ctx'), may hold values from -8 to 8
- prefill_query: bfloat16 [4096, 64, 192], P('ctx', 'head'), may hold values from -12 to 12
- span_start: int32 [1], replicated, may hold values from 0 to 2048
- w_uk: bfloat16 [64, 128, 512], P('head'), may hold values from -0.5 to 0.5
- w_uv: bfloat16 [64, 512, 128], P('head'), may hold values from -0.25 to 0.25
- decode_latent: bfloat16 [256, 256, 576], P(None, 'ctx'), may hold values from -8 to 8
- owner_slot: int32 [256], replicated, may hold values from 0 to 255, each once
- lengths: int32 [256], P('ctx'), may hold values from 1 to 256
- hidden_new: bfloat16 [4, 256, 7168], P(None, 'ctx', 'head'), may hold values from -6 to 6
- decode_query: bfloat16 [4, 256, 64, 192], P(None, 'ctx', 'head'), may hold values from -12 to 12
- w_down: bfloat16 [7168, 576], P('head'), may hold values from -0.0625 to 0.0625
- kv_gain: float32 [512], replicated, may hold values from 0.5 to 1.5
Outputs:
- prefill_out: bfloat16 [4096, 64, 128], P('ctx', 'head')
- decode_out: bfloat16 [4, 256, 64, 128], P(None, 'ctx', 'head')
Inputs may be any that keep to these rules, and one draw needn't show every extreme that they name: span_start + 4096 <= 6144. `owner_slot`: each slot once.
All inputs are finite; a program needn't handle non-finite values.
Results may differ from a plain program's by a relative error of at most 0.014.
Values may be sent and summed in bfloat16 or wider, within the bound.
No kernel may reach another device: no remote copies, remote signals or barrier semaphores. Data moves between devices by JAX's collectives and lax.ppermute only.
A program may use at most 128 MiB of HBM per device.

v0:
```python
import jax
import jax.numpy as jnp
from jax import lax
from jax.sharding import PartitionSpec as P

KV_RANK = 512
ROPE = 64
NOPE = 128


def gathered_total(array, axis):
    return lax.all_gather(array, axis).astype(jnp.float32).sum(0)


def absorb(query, w_uk, form):
    absorbed = jnp.einsum(form, query[..., :NOPE], w_uk, preferred_element_type=jnp.float32).astype(
        jnp.bfloat16
    )
    return jnp.concatenate([absorbed, query[..., NOPE:]], axis=-1)


def body(
    prompt_latent,
    prefill_query,
    span_start,
    w_uk,
    w_uv,
    decode_latent,
    owner_slot,
    lengths,
    hidden_new,
    decode_query,
    w_down,
    kv_gain,
):
    scale = (NOPE + ROPE) ** (-0.5)
    heads_here = w_uk.shape[0]
    queries = prefill_query.shape[0]
    width = prompt_latent.shape[1]
    full_query = absorb(prefill_query, w_uk, "qhn,hnc->qhc")
    rows = full_query.reshape(queries * heads_here, width)
    first = span_start[0] + lax.axis_index("ctx") * queries
    positions = jnp.repeat(first + jnp.arange(queries, dtype=jnp.int32), heads_here)
    count = rows.shape[0]
    piece = lax.all_gather(prompt_latent, "ctx", axis=0, tiled=True)
    top = jnp.full((count,), -1e30, jnp.float32)
    scores = jnp.dot(rows, piece.T, preferred_element_type=jnp.float32) * scale
    keys = jnp.arange(piece.shape[0], dtype=jnp.int32)
    allowed = keys[None, :] <= positions[:, None]
    peak = jnp.maximum(top, jnp.max(jnp.where(allowed, scores, -1e30), axis=1))
    probs = jnp.where(allowed, jnp.exp(scores - peak[:, None]), 0.0)
    total = jnp.sum(probs, axis=1)
    acc = jnp.dot(
        probs.astype(jnp.bfloat16), piece[:, :KV_RANK], preferred_element_type=jnp.float32
    )
    top, total, acc = (peak, total, acc)
    mixed = (acc / total[:, None]).astype(jnp.bfloat16).reshape(queries, heads_here, KV_RANK)
    prefill_out = jnp.einsum(
        "qhc,hcv->qhv", mixed, w_uv, preferred_element_type=jnp.float32
    ).astype(jnp.bfloat16)
    order = jnp.argsort(owner_slot)
    by_slot = decode_latent[order]
    cache = lax.all_to_all(by_slot, "ctx", split_axis=0, concat_axis=1, tiled=True)
    steps_here, owned, model_cols = hidden_new.shape
    raw_part = jnp.dot(
        hidden_new.reshape(steps_here * owned, model_cols),
        w_down,
        preferred_element_type=jnp.float32,
    )
    raw = gathered_total(raw_part.astype(jnp.bfloat16), "head").astype(jnp.float32)
    front = raw[:, :KV_RANK]
    factor = lax.rsqrt(jnp.mean(front * front, axis=1) + 1e-06)
    normed = front * factor[:, None] * kv_gain[None, :]
    new_rows = jnp.concatenate([normed, raw[:, KV_RANK:]], axis=1).astype(jnp.bfloat16)
    new_latent = new_rows.reshape(steps_here, owned, width)
    query = absorb(decode_query, w_uk, "srhn,hnc->srhc")
    cache_scores = (
        jnp.einsum("srhc,rjc->srhj", query, cache, preferred_element_type=jnp.float32) * scale
    )
    new_scores = (
        jnp.einsum("srhc,trc->srht", query, new_latent, preferred_element_type=jnp.float32) * scale
    )
    capacity = cache.shape[1]
    cache_ok = (jnp.arange(capacity, dtype=jnp.int32)[None, :] < lengths[:, None])[None, :, None, :]
    steps_idx = jnp.arange(steps_here, dtype=jnp.int32)
    new_ok = (steps_idx[None, :] <= steps_idx[:, None])[:, None, None, :]
    peak = jnp.maximum(
        jnp.max(jnp.where(cache_ok, cache_scores, -1e30), axis=3),
        jnp.max(jnp.where(new_ok, new_scores, -1e30), axis=3),
    )
    cache_p = jnp.where(cache_ok, jnp.exp(cache_scores - peak[..., None]), 0.0)
    new_p = jnp.where(new_ok, jnp.exp(new_scores - peak[..., None]), 0.0)
    total_d = jnp.sum(cache_p, axis=3) + jnp.sum(new_p, axis=3)
    mixed_d = jnp.einsum(
        "srhj,rjc->srhc",
        cache_p.astype(jnp.bfloat16),
        cache[:, :, :KV_RANK],
        preferred_element_type=jnp.float32,
    )
    mixed_d = mixed_d + jnp.einsum(
        "srht,trc->srhc",
        new_p.astype(jnp.bfloat16),
        new_latent[:, :, :KV_RANK],
        preferred_element_type=jnp.float32,
    )
    mixed_d = (mixed_d / total_d[..., None]).astype(jnp.bfloat16)
    decode_out = jnp.einsum(
        "srhc,hcv->srhv", mixed_d, w_uv, preferred_element_type=jnp.float32
    ).astype(jnp.bfloat16)
    return (prefill_out, decode_out)


def solution(mesh):
    in_specs = (
        P("ctx", None),
        P("ctx", "head", None),
        P(),
        P("head", None, None),
        P("head", None, None),
        P(None, "ctx", None),
        P(),
        P("ctx"),
        P(None, "ctx", "head"),
        P(None, "ctx", "head", None),
        P("head", None),
        P(),
    )
    out_specs = (P("ctx", "head", None), P(None, "ctx", "head", None))
    return jax.shard_map(body, mesh=mesh, in_specs=in_specs, out_specs=out_specs, check_vma=False)
```

profile of v0, /device:TPU:1, one launch (start us, length us, event | category | flops | bytes accessed | tf_op | source)
XLA Modules:
  0.0 162.7 jit_solution(17670993804524702445)
XLA Ops:
  7.2 0.0 copy-start
  7.2 0.0 all-gather.3.cloned.1.call-start
  7.2 0.7 all-gather.3.cloned.1.call-update
  7.9 2.8 %copy.43 = bf16[256,4,576]{2,1,0:T(4,128)(2,1)S(1)} copy(bf16[256,4,576]{0,2,1:T(8,128)(2,1)} %param.17) | data formatting | bytes 2359296 | tf_op args[5]
  10.7 0.0 copy-start.1
  10.7 3.9 %sort.17 = (s32[256]{0:T(256)}, s32[256]{0:T(256)S(1)}) sort(s32[256]{0:T(256)} %param.18, s32[256]{0:T(256)S(1)} %iota.33), dimensions={0}, to_apply=%region_2.3 | sort | flops 2048 | bytes 4096 | tf_op jit(solution)/shard_map/jit(argsort)/sort | solution.py:61
  14.7 2.9 %gather_fusion = bf16[256,4,576]{2,1,0:T(4,128)(2,1)} fusion(bf16[256,4,576]{2,1,0:T(4,128)(2,1)S(1)} %copy.43, s32[1024]{0:T(1024)S(1)} %pad_clamp_fusion), kind=kCustom, calls=%fused_computation | custom fusion | bytes 2360320 | tf_op jit(solution)/shard_map/gather | solution.py:62
  17.6 17.6 %all-to-all-start = ((bf16[256,4,576]{2,1,0:T(4,128)(2,1)}), bf16[256,4,576]{2,1,0:T(4,128)(2,1)S(1)}, u32[]{:S(2)}, u32[]{:S(2)}) async-start(bf16[256,4,576]{2,1,0:T(4,128)(2,1)} %gather_fusion), calls=%async_computation | async-start | bytes 2621440 | tf_op jit(solution)/shard_map/all_to_all | solution.py:63
  35.2 1.6 slice.27
  36.8 1.6 slice.26
  38.4 1.4 slice.31
  39.7 1.4 slice.30
  41.8 0.1 broadcast_in_dim.68
  41.8 0.7 le.39
  42.5 0.9 copy.68
  43.4 1.4 copy.71
  44.8 1.4 reshape.70
  46.2 1.6 convolution_convert_fusion.4
  47.8 35.9 %all-gather = bf16[128,576]{1,0:T(8,128)(2,1)S(1)} all-gather(bf16[16,576]{1,0:T(8,128)(2,1)S(1)} %convolution_convert_fusion.4), channel_id=2, replica_groups=mesh['ctx'=64,'head'=8] {'head'}, dimensions={0}, use_global_device_ids=true | all-gather | bytes 165888 | tf_op jit(solution)/shard_map/all_gather | solution.py:12
  83.7 0.6 copy.51
  84.3 0.1 multiply_reduce_fusion
  84.4 0.8 multiply_convert_fusion
  85.2 0.6 concatenate.17
  85.8 0.0 copy-start.3
  85.8 0.8 copy.50
  86.6 0.0 copy-done
  86.6 0.0 copy-start.5
  86.6 1.0 fusion.14
  87.6 0.8 pad_maximum_fusion.1
  88.5 0.0 copy-start.2
  88.5 1.3 fusion.10
  89.8 0.9 pad_maximum_fusion
  90.8 0.7 iota_compare_fusion.1
  91.5 0.0 copy-done.5
  91.5 0.0 copy-done.2
  91.5 1.2 select_reduce_fusion.2
  92.7 0.0 all-to-all-done
  92.7 0.5 copy.44
  93.3 0.4 slice.37
  93.6 1.5 select_reduce_fusion.1
  95.2 0.8 fusion.51
  95.9 0.2 fusion.44
  96.1 0.4 fusion.24
  96.5 0.0 copy-done.3
  96.5 1.0 fusion.13
  97.5 0.0 copy-done.1
  97.5 0.3 fusion.22
  97.8 0.6 copy.56
  98.5 0.0 copy-start.4
  98.5 37.6 %all-gather.3.cloned.1.call-done = bf16[6144,576]{1,0:T(8,128)(2,1)} async-done(((bf16[96,576]{1,0:T(8,128)(2,1)}), bf16[6144,576]{1,0:T(8,128)(2,1)}) %all-gather.3.cloned.1.call-update) | async-done | bytes 7077904 | tf_op jit(solution)/shard_map/all_gather | solution.py:45
  136.0 8.4 %select_reduce_fusion = (f32[512]{0:T(512)S(1)}, f32[512,6144]{1,0:T(8,128)S(1)}) fusion(s32[512]{0:T(512)} %le.39, bf16[6144,576]{1,0:T(8,128)(2,1)} %all-gather.3.cloned.1.call-done, bf16[64,8,576]{2,0,1:T(8,128)(2,1)} %pad_maximum_fusion), kind=kOutput, calls=%fused_computation.2 | convolution fusion | flops 3636461056 | bytes 20254720 | tf_op jit(solution)/shard_map/dot_general | solution.py:47
  144.5 0.0 copy-done.4
  144.5 3.7 %fusion = f32[512]{0:T(512)S(1)} fusion(f32[512,6144]{1,0:T(8,128)S(1)} %get-tuple-element.11, f32[512]{0:T(512)S(1)} %broadcast_maximum_fusion, s32[512]{0:T(512)S(1)} %copy-done.4), kind=kLoop, calls=%fused_computation.4 | loop fusion | flops 15728128 | bytes 12589056 | tf_op jit(solution)/shard_map/reduce_sum | solution.py:52
  148.1 6.5 %fusion.31 = bf16[64,8,512]{2,1,0:T(8,128)(2,1)S(1)} fusion(bf16[6144,576]{1,0:T(8,128)(2,1)} %all-gather.3.cloned.1.call-done, f32[512,6144]{1,0:T(8,128)S(1)} %get-tuple-element.11, f32[512]{0:T(512)S(1)} %broadcast_maximum_fusion, s32[512]{0:T(512)S(1)} %copy-done.4, f32[512]{0:T(512)S(1)} %fusion), kind=kOutput, calls=%fused_computation.35 | convolution fusion | flops 3237478400 | bytes 19404800 | tf_op jit(solution)/shard_map/dot_general | solution.py:53
  154.7 0.4 fusion.15
  155.1 0.7 copy.55
  (11 shorter events, 0.1 us)
Async XLA Ops:
  7.2 79.4 %copy-start = (bf16[8,128,512]{2,1,0:T(8,128)(2,1)S(1)}, bf16[8,128,512]{2,1,0:T(8,128)(2,1)}, u32[]{:S(2)}) copy-start(bf16[8,128,512]{2,1,0:T(8,128)(2,1)} %param.15) | copy-start | bytes 3145732
  7.2 128.8 %all-gather.3.cloned.1.call-start = ((), (), s32[]{:S(2)}) async-start(), calls=%async_computation.1 | async-start | bytes 7987200 | tf_op jit(solution)/shard_map/all_gather | solution.py:45
  10.7 86.8 %copy-start.1 = (bf16[8,512,128]{2,1,0:T(8,128)(2,1)S(1)}, bf16[8,512,128]{2,1,0:T(8,128)(2,1)}, u32[]{:S(2)}) copy-start(bf16[8,512,128]{2,1,0:T(8,128)(2,1)} %param.16) | copy-start | bytes 3145732
  17.6 75.1 %all-to-all-start = ((bf16[256,4,576]{2,1,0:T(4,128)(2,1)}), bf16[256,4,576]{2,1,0:T(4,128)(2,1)S(1)}, u32[]{:S(2)}, u32[]{:S(2)}) async-start(bf16[256,4,576]{2,1,0:T(4,128)(2,1)} %gather_fusion), calls=%async_computation | async-start | bytes 2621440 | tf_op jit(solution)/shard_map/all_to_all | solution.py:63
  85.8 10.7 %copy-start.3 = (bf16[4,4,512]{2,1,0:T(4,128)(2,1)S(1)}, bf16[4,4,512]{2,1,0:T(4,128)(2,1)}, u32[]{:S(2)}) copy-start(bf16[4,4,512]{2,1,0:T(4,128)(2,1)} %concatenate.17) | copy-start | bytes 49156
  86.6 4.9 %copy-start.5 = (pred[4,4]{1,0:T(4,128)(4,1)}, pred[4,4]{1,0:T(4,128)(4,1)S(1)}, u32[]{:S(2)}) copy-start(pred[4,4]{1,0:T(4,128)(4,1)S(1)} %iota_compare_fusion.2) | copy-start | bytes 52
  88.5 3.0 %copy-start.2 = (bf16[4,4,8,576]{3,1,0,2:T(4,128)(2,1)}, bf16[4,4,8,576]{3,1,0,2:T(4,128)(2,1)S(1)}, u32[]{:S(2)}) copy-start(bf16[4,4,8,576]{3,1,0,2:T(4,128)(2,1)S(1)} %pad_maximum_fusion.1) | copy-start | bytes 442372
  98.5 46.0 %copy-start.4 = (s32[512]{0:T(512)S(1)}, s32[512]{0:T(512)}, u32[]{:S(2)}) copy-start(s32[512]{0:T(512)} %le.39) | copy-start | bytes 6148
Sparse Core Ops, SparseCore 0:
  11.3 124.6 all-gather.2
where the time goes:
time: 164 us; the launch traced here: 163 us
  waiting for transfers between devices  38.2 us (23%)
  blocking collectives  35.9 us (22%)
  matrix products  23.7 us (14%)
  local copies, waits for them, and re-layouts  20.3 us (12%)
  starting transfers between devices  17.7 us (11%)
  between operations  14.9 us (9%)
  other arithmetic  12 us (7%)
    all_gather x1, waiting for transfers between devices, body(): piece = lax.all_gather(prompt_latent, 'ctx', axis=0, tiled=True)  37.6 us
    all_gather x1, blocking collectives, gathered_total(): return lax.all_gather(array, axis).astype(jnp.float32).sum(0)  35.9 us
    all_to_all x1, starting transfers between devices, body(): lax.all_to_all(by_slot, 'ctx', split_axis=0, concat_axis=1, tiled=True)  17.6 us
    dot_general x1, matrix products, body(): scores = jnp.dot(rows, piece.T, preferred_element_type=jnp.float32) * scale  8.44 us
    dot_general x1, matrix products, body(): jnp.dot(probs.astype(jnp.bfloat16), piece[:, :KV_RANK], preferred_element...  6.52 us
    unnamed x17, local copies, waits for them, and re-layouts  6.51 us
    sort x1, other arithmetic, body(): order = jnp.argsort(owner_slot)  3.92 us
    reduce_sum x1, other arithmetic, body(): total = jnp.sum(probs, axis=1)  3.65 us
  transfers between devices with their start and end apart: 2, of which 1 were waited for; matrix products, arithmetic and copies ran while one was open for 22% of the time, Pallas kernels for 0%

commit v1 on v0

--- a/solution.py
+++ b/solution.py
@@ -42,7 +42,9 @@
     first = span_start[0] + lax.axis_index("ctx") * queries
     positions = jnp.repeat(first + jnp.arange(queries, dtype=jnp.int32), heads_here)
     count = rows.shape[0]
-    piece = lax.all_gather(prompt_latent, "ctx", axis=0, tiled=True)
+    piece = jnp.concatenate(
+        lax.all_to_all(jnp.stack([prompt_latent] * lax.axis_size("ctx")), "ctx", 0, 0), axis=0
+    )
     top = jnp.full((count,), -1e30, jnp.float32)
     scores = jnp.dot(rows, piece.T, preferred_element_type=jnp.float32) * scale
     keys = jnp.arange(piece.shape[0], dtype=jnp.int32)

time: 164 us -> 357 us (2.18); the launches traced: 163 us -> 351 us
  blocking collectives: 35.9 us -> 286 us
  waiting for transfers between devices: 38.2 us -> 0.01 us
  between operations: 14.9 us -> 1.5 us
  starting transfers between devices: 17.7 us -> 8.82 us
    all_gather x1, blocking collectives: 35.9 us -> 228 us  [gathered_total(): return lax.all_gather(array, axis).astype(jnp.float32).sum(0)]
    all_to_all x0 -> x1, blocking collectives: none -> 58 us  [body(): lax.all_to_all(by_slot, 'ctx', split_axis=0, concat_axis=1, tiled=True)]
    all_gather x1 -> x0, waiting for transfers between devices: 37.6 us -> none  [body(): piece = lax.all_gather(prompt_latent, 'ctx', axis=0, tiled=True)]
    all_to_all x1, starting transfers between devices: 17.6 us -> 8.82 us  [body(): lax.all_to_all(jnp.stack([prompt_latent] * lax.axis_size('ctx')), 'ctx',...]
    another operation x0 -> x1, local copies, waits for them, and re-layouts: none -> 4.67 us  [body(): jnp.stack([prompt_latent] * lax.axis_size('ctx'))]
  transfers between devices with their start and end apart: 2 -> 1, of which waited for: 1 -> 0; matrix products, arithmetic and copies ran while one was open for 22% -> 6% of each run, Pallas kernels for 0% -> 0%
where the time goes in v1:
time: 357 us; the launch traced here: 351 us
  blocking collectives  286 us (80%)
  matrix products  22.2 us (6%)
  local copies, waits for them, and re-layouts  22.1 us (6%)
  other arithmetic  10.5 us (3%)
  starting transfers between devices  8.82 us (2%)
    all_gather x1, blocking collectives, gathered_total(): return lax.all_gather(array, axis).astype(jnp.float32).sum(0)  228 us
    all_to_all x1, blocking collectives, body(): lax.all_to_all(by_slot, 'ctx', split_axis=0, concat_axis=1, tiled=True)  58 us
    dot_general x1, matrix products, body(): scores = jnp.dot(rows, piece.T, preferred_element_type=jnp.float32) * scale  9.04 us
    all_to_all x1, starting transfers between devices, body(): lax.all_to_all(jnp.stack([prompt_latent] * lax.axis_size('ctx')), 'ctx',...  8.82 us
  transfers between devices with their start and end apart: 1, of which 0 were waited for; matrix products, arithmetic and copies ran while one was open for 6% of the time, Pallas kernels for 0%

profile of v1, /device:TPU:1, one launch (start us, length us, event | category | flops | bytes accessed | tf_op | source)
XLA Modules:
  0.0 351.1 jit_solution(125892703991407364)
XLA Ops:
  0.6 0.0 copy-start
  0.6 2.9 copy.43
  3.5 3.8 %sort.17 = (s32[256]{0:T(256)}, s32[256]{0:T(256)S(1)}) sort(s32[256]{0:T(256)} %param.18, s32[256]{0:T(256)S(1)} %iota.33), dimensions={0}, to_apply=%region_2.3 | sort | flops 2048 | bytes 4096 | tf_op jit(solution)/shard_map/jit(argsort)/sort | solution.py:63
  7.4 2.8 gather_fusion
  10.2 58.0 %all_to_all.23 = bf16[256,4,576]{2,1,0:T(4,128)(2,1)S(1)} all-to-all(bf16[256,4,576]{2,1,0:T(4,128)(2,1)} %gather_fusion), channel_id=1, replica_groups=mesh['ctx'=64,'head'=8] {'ctx'}, dimensions={0} | all-to-all | bytes 2359296 | tf_op jit(solution)/shard_map/all_to_all | solution.py:65
  68.2 4.7 %stack.2 = bf16[64,96,576]{2,1,0:T(8,128)(2,1)} broadcast(bf16[96,576]{1,0:T(8,128)(2,1)} %param.12), dimensions={1,2} | broadcast | bytes 7188480 | tf_op jit(solution)/shard_map/stack | solution.py:46
  72.9 0.0 copy-start.4
  72.9 0.0 copy-start.2
  72.9 0.0 copy-start.6
  72.9 8.8 %all-to-all-start = ((bf16[64,96,576]{2,1,0:T(8,128)(2,1)}), bf16[64,96,576]{2,1,0:T(8,128)(2,1)}, u32[]{:S(2)}, u32[]{:S(2)}) async-start(bf16[64,96,576]{2,1,0:T(8,128)(2,1)} %stack.2), calls=%async_computation | async-start | bytes 15728640 | tf_op jit(solution)/shard_map/all_to_all | solution.py:46
  81.7 1.6 slice.27
  83.3 1.6 slice.26
  84.9 0.0 copy-done.4
  84.9 0.6 slice.31
  85.5 0.6 slice.30
  86.8 0.1 broadcast_in_dim.68
  86.8 0.7 le.39
  87.5 0.9 copy.68
  88.4 1.4 copy.71
  89.8 1.4 reshape.76
  91.2 0.0 copy-done.2
  91.2 1.1 convolution_convert_fusion.4
  92.3 228.0 %all-gather = bf16[128,576]{1,0:T(8,128)(2,1)S(1)} all-gather(bf16[16,576]{1,0:T(8,128)(2,1)S(1)} %convolution_convert_fusion.4), channel_id=2, replica_groups=mesh['ctx'=64,'head'=8] {'head'}, dimensions={0}, use_global_device_ids=true | all-gather | bytes 165888 | tf_op jit(solution)/shard_map/all_gather | solution.py:12
  320.3 0.6 copy.51
  320.9 0.1 multiply_reduce_fusion
  321.0 0.0 copy-done.6
  321.0 0.1 multiply_convert_fusion
  321.2 0.0 copy-done
  321.2 0.0 copy-start.1
  321.2 1.1 fusion.14
  322.3 0.8 pad_maximum_fusion.1
  323.1 1.2 fusion.10
  324.3 0.9 pad_maximum_fusion
  325.3 0.7 iota_compare_fusion.1
  326.0 1.2 select_reduce_fusion.2
  327.2 0.5 copy.44
  327.8 0.0 copy-start.3
  327.8 0.4 slice.37
  328.1 0.6 select_reduce_fusion.1
  328.7 0.1 fusion.51
  328.8 0.2 fusion.44
  329.0 0.4 fusion.24
  329.5 0.3 fusion.13
  329.8 0.0 copy-done.1
  329.8 0.3 fusion.22
  330.1 0.6 copy.56
  330.7 0.0 all-to-all-done
  330.7 0.0 copy-done.3
  330.7 0.0 copy-start.5
  330.7 9.0 %select_reduce_fusion = (f32[512]{0:T(512)S(1)}, f32[512,6144]{1,0:T(8,128)S(1)}) fusion(s32[512]{0:T(512)} %le.39, bf16[6144,576]{1,0:T(8,128)(2,1)} %bitcast.3, bf16[64,8,576]{2,0,1:T(8,128)(2,1)S(1)} %copy-done.3), kind=kOutput, calls=%fused_computation.2 | convolution fusion | flops 3636461056 | bytes 20254720 | tf_op jit(solution)/shard_map/dot_general | solution.py:49
  339.8 0.0 copy-done.5
  339.8 3.7 %fusion = f32[512]{0:T(512)S(1)} fusion(f32[512,6144]{1,0:T(8,128)S(1)} %get-tuple-element.11, f32[512]{0:T(512)S(1)} %broadcast_maximum_fusion, s32[512]{0:T(512)S(1)} %copy-done.5), kind=kLoop, calls=%fused_computation.4 | loop fusion | flops 15728128 | bytes 12589056 | tf_op jit(solution)/shard_map/reduce_sum | solution.py:54
  343.4 6.5 %fusion.31 = bf16[64,8,512]{2,1,0:T(8,128)(2,1)S(1)} fusion(bf16[6144,576]{1,0:T(8,128)(2,1)} %bitcast.3, f32[512,6144]{1,0:T(8,128)S(1)} %get-tuple-element.11, f32[512]{0:T(512)S(1)} %broadcast_maximum_fusion, s32[512]{0:T(512)S(1)} %copy-done.5, f32[512]{0:T(512)S(1)} %fusion), kind=kOutput, calls=%fused_computation.35 | convolution fusion | flops 3237478400 | bytes 19404800 | tf_op jit(solution)/shard_map/dot_general | solution.py:55
  350.0 0.4 fusion.15
  350.4 0.7 copy.55
  (13 shorter events, 0.1 us)
Async XLA Ops:
  0.6 320.5 %copy-start = (bf16[8,128,512]{2,1,0:T(8,128)(2,1)S(1)}, bf16[8,128,512]{2,1,0:T(8,128)(2,1)}, u32[]{:S(2)}) copy-start(bf16[8,128,512]{2,1,0:T(8,128)(2,1)} %param.15) | copy-start | bytes 3145732
  72.9 12.0 %copy-start.4 = (bf16[4,4,8,192]{3,2,1,0:T(8,128)(2,1)S(1)}, bf16[4,4,8,192]{3,2,1,0:T(8,128)(2,1)}, u32[]{:S(2)}) copy-start(bf16[4,4,8,192]{3,2,1,0:T(8,128)(2,1)} %param.21) | copy-start | bytes 147460
  72.9 18.3 %copy-start.2 = (bf16[896,576]{0,1:T(8,128)(2,1)S(1)}, bf16[896,576]{0,1:T(8,128)(2,1)}, u32[]{:S(2)}) copy-start(bf16[896,576]{0,1:T(8,128)(2,1)} %param.22) | copy-start | bytes 3096580
  72.9 248.1 %copy-start.6 = (f32[512]{0:T(512)S(1)}, f32[512]{0:T(512)}, u32[]{:S(2)}) copy-start(f32[512]{0:T(512)} %param.23) | copy-start | bytes 6148
  72.9 257.8 %all-to-all-start = ((bf16[64,96,576]{2,1,0:T(8,128)(2,1)}), bf16[64,96,576]{2,1,0:T(8,128)(2,1)}, u32[]{:S(2)}, u32[]{:S(2)}) async-start(bf16[64,96,576]{2,1,0:T(8,128)(2,1)} %stack.2), calls=%async_computation | async-start | bytes 15728640 | tf_op jit(solution)/shard_map/all_to_all | solution.py:46
  321.2 8.6 %copy-start.1 = (bf16[8,512,128]{2,1,0:T(8,128)(2,1)S(1)}, bf16[8,512,128]{2,1,0:T(8,128)(2,1)}, u32[]{:S(2)}) copy-start(bf16[8,512,128]{2,1,0:T(8,128)(2,1)} %param.16) | copy-start | bytes 3145732
  327.8 3.0 copy-start.3
  330.7 9.1 %copy-start.5 = (s32[512]{0:T(512)S(1)}, s32[512]{0:T(512)}, u32[]{:S(2)}) copy-start(s32[512]{0:T(512)} %le.39) | copy-start | bytes 6148
